TPU v7x, 32 devices: a whole 2x2x4 slice. The times are simulated.
32 devices in a mesh: dp: 16 (over z, x, core), rep: 2 (over y).
Axes of the slice: x: 2, y: 2, z: 4, core: 2. Of those that a mesh axis runs over, the one named last changes fastest.
Arguments:
- learn_residual: bfloat16 [20480, 1024], P(('dp', 'rep')), may hold values from -6 to 6
- learn_hidden: bfloat16 [20480, 4096], P(('dp', 'rep')), may hold values from -6 to 6
- fresh_residual: bfloat16 [20480, 1024], P(('dp', 'rep')), may hold values from -6 to 6
- fresh_hidden: bfloat16 [20480, 4096], P(('dp', 'rep')), may hold values from -6 to 6
- down_weight: bfloat16 [4096, 1024], P('dp'), may hold values from -0.09375 to 0.09375
- head_weight: bfloat16 [1024, 19], replicated, may hold values from -0.1875 to 0.1875
- norm_gain: bfloat16 [1024], replicated, may hold values from 0.099609375 to 1.8984375
- actions: int32 [256, 80], P(('dp', 'rep')), may hold values from 0 to 17
- behaviour_logits: float32 [20480, 18], P(('dp', 'rep')), may hold values from -6 to 6
- rewards: float32 [256, 80], P(('dp', 'rep')), may hold values from -6 to 6
- episode_done: int32 [256, 80], P(('dp', 'rep')), may hold values 0 or 1
- lengths: int32 [256], P(('dp', 'rep')), may hold values from 40 to 80, as said below
- bootstrap: float32 [256], P(('dp', 'rep')), may hold values from -6 to 6
Outputs:
- fresh_policy: float32 [20480, 19], P(('dp', 'rep'))
- learn_targets: float32 [256, 80], P(('dp', 'rep'))
- hidden_grad: bfloat16 [20480, 4096], P(('dp', 'rep'))
- down_grad: float32 [4096, 1024], P('dp')
- head_grad: float32 [1024, 19], replicated
- gain_grad: float32 [1024], replicated
Inputs may be any that keep to these rules, and one draw needn't show every extreme that they name: `lengths`: on at least one device all 8 trajectories of that device have the full 80 steps.
All inputs are finite; a program needn't handle non-finite values. No bound on the sum of `episode_done` on one device may be relied on, other than what follows from the above.
Results may differ from a plain program's by a relative error of at most 0.0049.
Values may be sent and summed in bfloat16 or wider, within the bound.
A program may use at most 128 MiB of HBM per device.

v0:
```python
import jax
import jax.numpy as jnp
from jax import lax
from jax.sharding import PartitionSpec as P

ACTIONS = 18
STEPS = 80
TRAJ_DEV = 8
DISCOUNT = 0.99
BASELINE_COST = 0.5
ENTROPY_COST = 0.05
EPSILON = 1e-05


def normalize(features, gain_vector):
    inverse_rms = lax.rsqrt(jnp.mean(features * features, axis=1, keepdims=True) + EPSILON)
    return features * inverse_rms * gain_vector[None, :]


def head_outputs(features, head_matrix, gain_vector):
    return jnp.dot(normalize(features, gain_vector), head_matrix, precision=lax.Precision.HIGHEST)


def log_policy(logits):
    return logits - jnp.log(jnp.sum(jnp.exp(logits), axis=-1, keepdims=True))


def compose_steps(earlier, later):
    return (earlier[0] * later[0], later[1] + later[0] * earlier[1])


def trace_returns(errors, traces):
    _, corrections = lax.associative_scan(compose_steps, (traces, errors), reverse=True, axis=1)
    return corrections


def learner_loss(
    features,
    head_matrix,
    gain_vector,
    actions,
    behaviour_logits,
    rewards,
    episode_done,
    lengths,
    bootstrap,
):
    trajectories = actions.shape[0]
    outputs = head_outputs(features, head_matrix, gain_vector)
    logprob = log_policy(outputs[:, :ACTIONS])
    values = outputs[:, ACTIONS].reshape(trajectories, STEPS)
    one_hot = (
        actions.reshape(-1)[:, None] == jnp.arange(ACTIONS, dtype=jnp.int32)[None, :]
    ).astype(jnp.float32)
    taken = jnp.sum(logprob * one_hot, axis=1).reshape(trajectories, STEPS)
    behaved = jnp.sum(log_policy(behaviour_logits) * one_hot, axis=1).reshape(trajectories, STEPS)
    entropy = -jnp.sum(jnp.exp(logprob) * logprob, axis=1).reshape(trajectories, STEPS)
    clipped_ratio = jnp.minimum(1.0, jnp.exp(lax.stop_gradient(taken) - behaved))
    positions = jnp.arange(STEPS, dtype=jnp.int32)[None, :]
    inside = positions < lengths[:, None]
    final_step = positions == lengths[:, None] - 1
    discounts = DISCOUNT * (1.0 - episode_done.astype(jnp.float32))
    baseline = lax.stop_gradient(values)
    empty_column = jnp.zeros((trajectories, 1), jnp.float32)
    next_value = jnp.concatenate([baseline[:, 1:], empty_column], axis=1)
    next_value = jnp.where(final_step, bootstrap[:, None], next_value)
    errors = jnp.where(inside, clipped_ratio * (rewards + discounts * next_value - baseline), 0.0)
    traces = jnp.where(inside, discounts * clipped_ratio, 0.0)
    targets = baseline + trace_returns(errors, traces)
    next_target = jnp.concatenate([targets[:, 1:], empty_column], axis=1)
    next_target = jnp.where(final_step, bootstrap[:, None], next_target)
    advantage = clipped_ratio * (rewards + discounts * next_target - baseline)
    per_step = (
        -advantage * taken + 0.5 * BASELINE_COST * (targets - values) ** 2 - ENTROPY_COST * entropy
    )
    total_loss = jnp.sum(jnp.where(inside, per_step, 0.0)) / (TRAJ_DEV * STEPS)
    return (total_loss, targets)


def local(
    learn_residual,
    learn_hidden,
    fresh_residual,
    fresh_hidden,
    down_weight,
    head_weight,
    norm_gain,
    actions,
    behaviour_logits,
    rewards,
    episode_done,
    lengths,
    bootstrap,
):
    head_matrix = head_weight.astype(jnp.float32)
    gain_vector = norm_gain.astype(jnp.float32)
    full_down = lax.all_gather(down_weight, "dp", axis=0, tiled=True)
    learn_stream = learn_residual.astype(jnp.float32) + jnp.dot(
        learn_hidden, full_down, preferred_element_type=jnp.float32
    )
    fresh_stream = fresh_residual.astype(jnp.float32) + jnp.dot(
        fresh_hidden, full_down, preferred_element_type=jnp.float32
    )
    fresh_policy = head_outputs(fresh_stream, head_matrix, gain_vector)

    def loss_of(features, head_values, gain_values):
        return learner_loss(
            features,
            head_values,
            gain_values,
            actions,
            behaviour_logits,
            rewards,
            episode_done,
            lengths,
            bootstrap,
        )

    total_loss, pullback, targets = jax.vjp(
        loss_of, learn_stream, head_matrix, gain_vector, has_aux=True
    )
    stream_grad, head_local, gain_local = pullback(jnp.ones_like(total_loss))
    rounded = stream_grad.astype(jnp.bfloat16)
    head_grad, gain_grad = lax.psum((head_local, gain_local), ("dp", "rep"))
    grad_shard = lax.psum_scatter(
        lax.dot_general(
            learn_hidden, rounded, (((0,), (0,)), ((), ())), preferred_element_type=jnp.float32
        ),
        "dp",
        scatter_dimension=0,
        tiled=True,
    )
    down_grad = lax.psum(grad_shard, "rep")
    hidden_sum = lax.dot_general(
        rounded, full_down, (((1,), (1,)), ((), ())), preferred_element_type=jnp.float32
    )
    hidden_grad = hidden_sum.astype(jnp.bfloat16)
    return (fresh_policy, targets, hidden_grad, down_grad, head_grad, gain_grad)


def solution(mesh):
    placed = (
        P(("dp", "rep"), None),
        P(("dp", "rep"), None),
        P(("dp", "rep"), None),
        P(("dp", "rep"), None),
        P("dp", None),
        P(),
        P(),
        P(("dp", "rep"), None),
        P(("dp", "rep"), None),
        P(("dp", "rep"), None),
        P(("dp", "rep"), None),
        P(("dp", "rep")),
        P(("dp", "rep")),
    )
    return jax.shard_map(
        local,
        mesh=mesh,
        in_specs=placed,
        out_specs=(
            P(("dp", "rep"), None),
            P(("dp", "rep"), None),
            P(("dp", "rep"), None),
            P("dp", None),
            P(),
            P(),
        ),
        check_vma=False,
    )
```

profile of v0, /device:TPU:8, one launch (start us, length us, event | category | flops | bytes accessed | tf_op | source)
XLA Modules:
  0.0 475.9 jit_solution(9676328896604979801)
XLA Ops:
  7.2 0.7 all-gather.2.cloned.1.call-update
  8.0 0.7 convert_element_type.21
  8.6 0.8 eq.12
  9.4 0.9 exponential_reduce_fusion
  10.3 0.7 broadcast_add_fusion
  10.9 74.4 %all-gather.2.cloned.1.call-done = bf16[4096,1024]{1,0:T(8,128)(2,1)} async-done(((bf16[256,1024]{1,0:T(8,128)(2,1)}), bf16[4096,1024]{1,0:T(8,128)(2,1)}) %all-gather.2.cloned.1.call-update) | async-done | bytes 8388624 | tf_op jit(solution)/shard_map/all_gather | solution.py:97
  85.4 9.9 %multiply_reduce_fusion.2 = (f32[640]{0:T(1024)S(1)}, f32[640,1024]{1,0:T(8,128)S(1)}) fusion(bf16[640,4096]{1,0:T(8,128)(2,1)} %param.14, bf16[4096,1024]{1,0:T(8,128)(2,1)} %all-gather.2.cloned.1.call-done, bf16[640,1024]{1,0:T(8,128)(2,1)} %param.13), kind=kOutput, calls=%fused_computation.6 | convolution fusion | flops 5371330048 | bytes 17566208 | tf_op jit(solution)/shard_map/dot_general | solution.py:98
  95.4 1.5 fusion.6
  97.4 0.1 slice.177
  97.5 0.1 slice.171
  97.6 0.1 slice.167
  97.7 0.1 slice.173
  97.8 0.1 slice.169
  98.2 0.1 slice.185
  100.2 0.1 slice.176
  100.3 0.1 slice.165
  101.7 0.1 pad.56
  102.0 0.1 pad.55
  102.7 1.8 multiply_reduce_fusion
  104.6 0.5 fusion
  105.1 1.2 copy-done.1
  106.3 12.7 %convolution_bitcast_fusion = f32[4096,1024]{0,1:T(8,128)} fusion(bf16[640,1024]{1,0:T(8,128)(2,1)S(1)} %fusion, bf16[640,4096]{1,0:T(8,128)(2,1)} %param.14), kind=kOutput, calls=%fused_computation | convolution fusion | flops 5368709120 | bytes 23330816 | tf_op jit(solution)/shard_map/dot_general | solution.py:126
  119.0 175.0 %reduce-scatter.2.cloned.1.call-done = f32[256,1024]{0,1:T(8,128)} async-done(((f32[4096,1024]{0,1:T(8,128)}), f32[256,1024]{0,1:T(8,128)}) %reduce-scatter.2.cloned.1.call-update) | async-done | bytes 1048592 | tf_op jit(solution)/shard_map/reduce_scatter | solution.py:125
  294.1 0.2 all-reduce.21.cloned.1.call-start
  294.3 10.9 %multiply_reduce_fusion.3 = (f32[640]{0:T(1024)S(1)}, f32[640,1024]{1,0:T(8,128)}) fusion(bf16[640,1024]{1,0:T(8,128)(2,1)} %param.15, bf16[640,4096]{1,0:T(8,128)(2,1)} %param.16, bf16[4096,1024]{1,0:T(8,128)(2,1)} %all-gather.2.cloned.1.call-done), kind=kOutput, calls=%fused_computation.11 | convolution fusion | flops 5371330048 | bytes 17566208 | tf_op jit(solution)/shard_map/dot_general | solution.py:101
  305.2 2.4 fusion.4
  307.6 11.1 %convolution_convert_fusion = bf16[640,4096]{1,0:T(8,128)(2,1)} fusion(bf16[640,1024]{1,0:T(8,128)(2,1)} %copy-done.1, bf16[4096,1024]{1,0:T(8,128)(2,1)} %all-gather.2.cloned.1.call-done), kind=kOutput, calls=%fused_computation.1 | convolution fusion | flops 5371330560 | bytes 14942208 | tf_op jit(solution)/shard_map/dot_general | solution.py:134
  318.8 2.3 fusion.1
  321.1 40.5 %psum.23 = f32[1024]{0:T(1024)} all-reduce(f32[1024]{0:T(1024)S(1)} %get-tuple-element.12), channel_id=1, replica_groups=mesh['dp'=16,'rep'=2] {'dp','rep'}, use_global_device_ids=true, to_apply=%region_12.13 | all-reduce | flops 1024 | bytes 8192 | tf_op jit(solution)/shard_map/psum | solution.py:124
  361.5 2.5 copy.19
  364.1 103.8 %all-reduce.21.cloned.1.call-done = f32[1024,19]{0,1:T(8,128)} async-done(((f32[1024,19]{0,1:T(8,128)}), f32[1024,19]{0,1:T(8,128)}) %all-reduce.21.cloned.1.call-update) | async-done | bytes 77840 | tf_op jit(solution)/shard_map/psum | solution.py:124
  467.8 1.5 copy.22
  (107 shorter events, 4.8 us)
Async XLA Ops:
  7.2 88.2 %copy-start = (bf16[1024,19]{0,1:T(8,128)(2,1)S(1)}, bf16[1024,19]{0,1:T(8,128)(2,1)}, u32[]{:S(2)}) copy-start(bf16[1024,19]{0,1:T(8,128)(2,1)} %param.18) | copy-start | bytes 116740
  7.2 78.2 %all-gather.2.cloned.1.call-start = ((), (), s32[]{:S(2)}) async-start(), calls=%async_computation.1 | async-start | bytes 8912896 | tf_op jit(solution)/shard_map/all_gather | solution.py:97
  7.9 286.2 %reduce-scatter.2.cloned.1.call-start = ((), (), s32[]{:S(2)}) async-start(), calls=%async_computation.2 | async-start | bytes 17825792 | tf_op jit(solution)/shard_map/reduce_scatter | solution.py:125
  95.3 1.8 copy-start.4
  95.3 2.0 copy-start.6
  95.3 1.9 copy-start.7
  95.3 1.9 copy-start.8
  95.3 1.9 copy-start.9
  102.3 2.3 copy-start.5
  105.1 1.2 copy-start.1
  119.0 242.5 %all-reduce.19.cloned.1.call-start = ((), (), s32[]{:S(2)}) async-start(), calls=%async_computation.3 | async-start | bytes 2097152 | tf_op jit(solution)/shard_map/psum | solution.py:133
  294.1 173.7 %all-reduce.21.cloned.1.call-start = ((), (), s32[]{:S(2)}) async-start(), calls=%async_computation.4 | async-start | bytes 196608 | tf_op jit(solution)/shard_map/psum | solution.py:124
  307.6 11.1 %copy-start.2 = (f32[640,1024]{1,0:T(8,128)S(1)}, f32[640,1024]{1,0:T(8,128)}, u32[]{:S(2)}) copy-start(f32[640,1024]{1,0:T(8,128)} %get-tuple-element.39) | copy-start | bytes 7864324
  307.6 11.1 %copy-start.3 = (bf16[640,1024]{1,0:T(8,128)(2,1)S(1)}, bf16[640,1024]{1,0:T(8,128)(2,1)}, u32[]{:S(2)}) copy-start(bf16[640,1024]{1,0:T(8,128)(2,1)} %param.15) | copy-start | bytes 3932164
Sparse Core Ops, SparseCore 0:
  10.2 75.1 all-gather.1
  119.1 174.9 reduce-scatter.1
  296.4 40.8 all-reduce.18
  343.2 124.5 all-reduce.20
where the time goes:
time: 476 us
  waiting for transfers between devices  354 us (74%)
  matrix products  52.6 us (11%)
  blocking collectives  40.5 us (9%)
  between operations  14.1 us (3%)
  local copies, waits for them, and re-layouts  10.6 us (2%)
    reduce_scatter x1, waiting for transfers between devices, local(): lax.psum_scatter(lax.dot_general(learn_hidden, rounded, (((0,), (0,)), ((...  175 us
    psum x1, waiting for transfers between devices, local(): head_grad, gain_grad = lax.psum((head_local, gain_local), ('dp', 'rep'))  104 us
    all_gather x1, waiting for transfers between devices, local(): full_down = lax.all_gather(down_weight, 'dp', axis=0, tiled=True)  74.4 us
    psum x1, blocking collectives, local(): head_grad, gain_grad = lax.psum((head_local, gain_local), ('dp', 'rep'))  40.5 us
    dot_general x1, matrix products, local(): lax.dot_general(learn_hidden, rounded, (((0,), (0,)), ((), ())), preferre...  12.7 us
    dot_general x1, matrix products, local(): lax.dot_general(rounded, full_down, (((1,), (1,)), ((), ())), preferred_e...  11.1 us
    dot_general x1, matrix products, local(): jnp.dot(fresh_hidden, full_down, preferred_element_type=jnp.float32)  10.9 us
    dot_general x1, matrix products, local(): jnp.dot(learn_hidden, full_down, preferred_element_type=jnp.float32)  9.89 us
  transfers between devices with their start and end apart: 4, of which 3 were waited for; matrix products, arithmetic and copies ran while one was open for 7% of the time, Pallas kernels for 0%

commit v1 on v0

--- a/solution.py
+++ b/solution.py
@@ -121,7 +121,7 @@
     )
     stream_grad, head_local, gain_local = pullback(jnp.ones_like(total_loss))
     rounded = stream_grad.astype(jnp.bfloat16)
-    head_grad, gain_grad = lax.psum((head_local, gain_local), ("dp", "rep"))
+    head_grad, gain_grad = lax.psum(lax.psum((head_local, gain_local), "rep"), "dp")
     grad_shard = lax.psum_scatter(
         lax.dot_general(
             learn_hidden, rounded, (((0,), (0,)), ((), ())), preferred_element_type=jnp.float32

time: 476 us -> 441 us (0.926)
  waiting for transfers between devices: 354 us -> 327 us
  blocking collectives: 40.5 us -> 29.4 us
    psum x1, waiting for transfers between devices: 104 us -> 56.3 us  [local(): lax.psum(lax.psum((head_local, gain_local), 'rep'), 'dp')]
    psum x1, waiting for transfers between devices: 0.01 us -> 34.2 us  [local(): down_grad = lax.psum(grad_shard, 'rep')]
    reduce_scatter x1, waiting for transfers between devices: 175 us -> 161 us  [local(): lax.psum_scatter(lax.dot_general(learn_hidden, rounded, (((0,), (0,)), ((...]
    psum x1 -> x2, blocking collectives: 40.5 us -> 29.4 us  [the longest x1 24.5 us: local(): lax.psum(lax.psum((head_local, gain_local), 'rep'), 'dp')]
  transfers between devices with their start and end apart: 4 -> 4, of which waited for: 3 -> 4; matrix products, arithmetic and copies ran while one was open for 7% -> 8% of each run, Pallas kernels for 0% -> 0%
where the time goes in v1:
time: 441 us; the launch traced here: 439 us
  waiting for transfers between devices  327 us (74%)
  matrix products  54 us (12%)
  blocking collectives  29.4 us (7%)
  between operations  14.1 us (3%)
  local copies, waits for them, and re-layouts  10.5 us (2%)
    reduce_scatter x1, waiting for transfers between devices, local(): lax.psum_scatter(lax.dot_general(learn_hidden, rounded, (((0,), (0,)), ((...  161 us
    all_gather x1, waiting for transfers between devices, local(): full_down = lax.all_gather(down_weight, 'dp', axis=0, tiled=True)  74.4 us
    psum x1, waiting for transfers between devices, local(): lax.psum(lax.psum((head_local, gain_local), 'rep'), 'dp')  56.3 us
    psum x1, waiting for transfers between devices, local(): down_grad = lax.psum(grad_shard, 'rep')  34.2 us
    psum x1, blocking collectives, local(): lax.psum(lax.psum((head_local, gain_local), 'rep'), 'dp')  24.5 us
    dot_general x1, matrix products, local(): lax.dot_general(learn_hidden, rounded, (((0,), (0,)), ((), ())), preferre...  12.7 us
    dot_general x1, matrix products, local(): lax.dot_general(rounded, full_down, (((1,), (1,)), ((), ())), preferred_e...  11.1 us
    dot_general x1, matrix products, local(): jnp.dot(fresh_hidden, full_down, preferred_element_type=jnp.float32)  11 us
  transfers between devices with their start and end apart: 4, of which 4 were waited for; matrix products, arithmetic and copies ran while one was open for 8% of the time, Pallas kernels for 0%

profile of v1, /device:TPU:8, one launch (start us, length us, event | category | flops | bytes accessed | tf_op | source)
XLA Modules:
  0.0 439.4 jit_solution(2903962940751762640)
XLA Ops:
  7.2 0.7 all-gather.2.cloned.1.call-update
  8.0 0.7 convert_element_type.21
  8.6 0.8 eq.12
  9.4 0.9 exponential_reduce_fusion
  10.3 0.7 broadcast_add_fusion
  10.9 74.4 %all-gather.2.cloned.1.call-done = bf16[4096,1024]{1,0:T(8,128)(2,1)} async-done(((bf16[256,1024]{1,0:T(8,128)(2,1)}), bf16[4096,1024]{1,0:T(8,128)(2,1)}) %all-gather.2.cloned.1.call-update) | async-done | bytes 8388624 | tf_op jit(solution)/shard_map/all_gather | solution.py:97
  85.4 9.9 %multiply_reduce_fusion.2 = (f32[640]{0:T(1024)S(1)}, f32[640,1024]{1,0:T(8,128)S(1)}) fusion(bf16[640,4096]{1,0:T(8,128)(2,1)} %param.14, bf16[4096,1024]{1,0:T(8,128)(2,1)} %all-gather.2.cloned.1.call-done, bf16[640,1024]{1,0:T(8,128)(2,1)} %param.13), kind=kOutput, calls=%fused_computation.6 | convolution fusion | flops 5371330048 | bytes 17566208 | tf_op jit(solution)/shard_map/dot_general | solution.py:98
  95.4 1.5 fusion.6
  97.4 0.1 slice.177
  97.5 0.1 slice.171
  97.6 0.1 slice.167
  97.7 0.1 slice.173
  97.8 0.1 slice.169
  100.2 0.1 slice.176
  100.3 0.1 slice.165
  102.0 0.1 pad.55
  102.7 1.8 multiply_reduce_fusion
  104.6 0.6 fusion
  105.2 1.1 copy-done.1
  106.2 12.7 %convolution_bitcast_fusion = f32[4096,1024]{0,1:T(8,128)} fusion(bf16[640,1024]{1,0:T(8,128)(2,1)S(1)} %fusion, bf16[640,4096]{1,0:T(8,128)(2,1)} %param.14), kind=kOutput, calls=%fused_computation | convolution fusion | flops 5368709120 | bytes 23330816 | tf_op jit(solution)/shard_map/dot_general | solution.py:126
  119.0 0.2 all-reduce.22.cloned.1.call-start
  119.2 11.0 %multiply_reduce_fusion.3 = (f32[640]{0:T(1024)S(1)}, f32[640,1024]{1,0:T(8,128)}) fusion(bf16[640,1024]{1,0:T(8,128)(2,1)} %param.15, bf16[640,4096]{1,0:T(8,128)(2,1)} %param.16, bf16[4096,1024]{1,0:T(8,128)(2,1)} %all-gather.2.cloned.1.call-done), kind=kOutput, calls=%fused_computation.11 | convolution fusion | flops 5371330048 | bytes 17566208 | tf_op jit(solution)/shard_map/dot_general | solution.py:101
  130.2 2.4 fusion.4
  132.6 161.5 %reduce-scatter.2.cloned.1.call-done = f32[256,1024]{0,1:T(8,128)} async-done(((f32[4096,1024]{0,1:T(8,128)}), f32[256,1024]{0,1:T(8,128)}) %reduce-scatter.2.cloned.1.call-update) | async-done | bytes 1048592 | tf_op jit(solution)/shard_map/reduce_scatter | solution.py:125
  294.2 11.1 %convolution_convert_fusion = bf16[640,4096]{1,0:T(8,128)(2,1)} fusion(bf16[640,1024]{1,0:T(8,128)(2,1)} %copy-done.1, bf16[4096,1024]{1,0:T(8,128)(2,1)} %all-gather.2.cloned.1.call-done), kind=kOutput, calls=%fused_computation.1 | convolution fusion | flops 5371330560 | bytes 14942208 | tf_op jit(solution)/shard_map/dot_general | solution.py:134
  305.2 34.2 %all-reduce.22.cloned.1.call-done = (f32[256,1024]{0,1:T(8,128)}, f32[1024,19]{0,1:T(8,128)}) async-done(((f32[256,1024]{0,1:T(8,128)}, f32[1024,19]{0,1:T(8,128)}), (f32[256,1024]{0,1:T(8,128)}, f32[1024,19]{0,1:T(8,128)})) %all-reduce.22.cloned.1.call-update) | async-done | bytes 1126416 | tf_op jit(solution)/shard_map/psum | solution.py:133
  339.5 3.6 fusion.1
  343.1 4.9 %psum.38 = f32[1024]{0:T(1024)S(1)} all-reduce(f32[1024]{0:T(1024)S(1)} %get-tuple-element.12), channel_id=1, replica_groups=mesh['dp'=16,'rep'=2] {'rep'}, use_global_device_ids=true, to_apply=%region_13.14 | all-reduce | flops 1024 | bytes 8192 | tf_op jit(solution)/shard_map/psum | solution.py:124
  348.0 24.5 %psum.39 = f32[1024]{0:T(1024)} all-reduce(f32[1024]{0:T(1024)S(1)} %psum.38), channel_id=1, replica_groups=mesh['dp'=16,'rep'=2] {'dp'}, use_global_device_ids=true, to_apply=%region_14.15 | all-reduce | flops 1024 | bytes 8192 | tf_op jit(solution)/shard_map/psum | solution.py:124
  372.5 2.5 copy.19
  375.1 56.3 %all-reduce.20.cloned.1.call-done = f32[1024,19]{0,1:T(8,128)} async-done(((f32[1024,19]{0,1:T(8,128)}), f32[1024,19]{0,1:T(8,128)}) %all-reduce.20.cloned.1.call-update) | async-done | bytes 77840 | tf_op jit(solution)/shard_map/psum | solution.py:124
  431.4 1.5 copy.23
  (106 shorter events, 5.0 us)
Async XLA Ops:
  7.2 88.2 %copy-start = (bf16[1024,19]{0,1:T(8,128)(2,1)S(1)}, bf16[1024,19]{0,1:T(8,128)(2,1)}, u32[]{:S(2)}) copy-start(bf16[1024,19]{0,1:T(8,128)(2,1)} %param.18) | copy-start | bytes 116740
  7.2 78.2 %all-gather.2.cloned.1.call-start = ((), (), s32[]{:S(2)}) async-start(), calls=%async_computation.1 | async-start | bytes 8912896 | tf_op jit(solution)/shard_map/all_gather | solution.py:97
  7.9 286.2 %reduce-scatter.2.cloned.1.call-start = ((), (), s32[]{:S(2)}) async-start(), calls=%async_computation.2 | async-start | bytes 17825792 | tf_op jit(solution)/shard_map/reduce_scatter | solution.py:125
  95.3 1.8 copy-start.3
  95.3 2.0 copy-start.5
  95.3 1.9 copy-start.6
  95.3 1.9 copy-start.7
  95.3 1.9 copy-start.8
  102.3 2.3 copy-start.4
  105.2 1.1 copy-start.1
  119.0 220.5 %all-reduce.22.cloned.1.call-start = ((), (), s32[]{:S(2)}) async-start(), calls=%async_computation.4 | async-start | bytes 2293760 | tf_op jit(solution)/shard_map/psum | solution.py:133
  294.1 45.4 %copy-start.2 = (f32[640,1024]{1,0:T(8,128)S(1)}, f32[640,1024]{1,0:T(8,128)}, u32[]{:S(2)}) copy-start(f32[640,1024]{1,0:T(8,128)} %get-tuple-element.41) | copy-start | bytes 7864324
  294.1 137.3 %all-reduce.20.cloned.1.call-start = ((), (), s32[]{:S(2)}) async-start(), calls=%async_computation.3 | async-start | bytes 196608 | tf_op jit(solution)/shard_map/psum | solution.py:124
Sparse Core Ops, SparseCore 0:
  10.2 75.1 all-gather.1
  119.1 174.9 reduce-scatter.1
  297.1 42.3 all-reduce.21
  342.7 88.5 all-reduce.19
